TPU v7x, 256 devices: a whole 4x4x8 slice. The times are simulated.
256 devices in a mesh: ctx: 16 (over y_hi, x, core), dp: 16 (over y_lo, z).
Axes of the slice: x: 4, y: 4 (y_hi: 2, y_lo: 2; y = y_hi * 2 + y_lo), z: 8, core: 2. Of those that a mesh axis runs over, the one named last changes fastest.
Arguments:
- queries: bfloat16 [16, 2048, 1536], P('dp', 'ctx'), as said below
- keys: bfloat16 [16, 2048, 1536], P('dp', 'ctx'), as said below
- values: bfloat16 [16, 2048, 1536], P('dp', 'ctx'), may hold values from -6 to 6
- tangent_queries: bfloat16 [16, 2048, 1536], P('dp', 'ctx'), may hold values from -6 to 6
- tangent_keys: bfloat16 [16, 2048, 1536], P('dp', 'ctx'), may hold values from -6 to 6
- tangent_values: bfloat16 [16, 2048, 1536], P('dp', 'ctx'), may hold values from -6 to 6
- clip_ids: int32 [16, 2048], P('dp', 'ctx'), may hold values from 0 to 3, never falling along the last dimension, each value on 1 to 1024 neighbouring positions
- block_order: int32 [16], replicated, may hold values from 0 to 15, each once
- out_weight: bfloat16 [1536, 3072], replicated, may hold values from -0.15625 to 0.15625
- layer_scale: float32 [3072], replicated, may hold values from 0.1 to 1.9
- cotangent: bfloat16 [16, 2048, 3072], P('dp', 'ctx'), as said below
Outputs:
- tangent_branch: bfloat16 [16, 2048, 3072], P('dp', 'ctx')
- scale_grad: float32 [3072], replicated
Inputs may be any that keep to these rules, and one draw needn't show every extreme that they name: `clip_ids`: ids never fall along a sample's rows; each of the 4 clips is a run of consecutive rows. `block_order`: each block number appears once. `queries`: real-valued. `keys`: real-valued. `cotangent`: real-valued.
All inputs are finite; a program needn't handle non-finite values.
Results may differ from a plain program's by a relative error of at most 0.02.
The roundings to bfloat16 on the way count: a program that leaves them out, or rounds other values in their place, can miss the bound.
Values may be sent and summed in bfloat16 or wider, within the bound.
A program may use at most 192 MiB of HBM per device.

v0:
```python
import math
import jax
import jax.numpy as jnp
from jax import lax
from jax.sharding import PartitionSpec as P

HEADS = 12


def rotate(x, pos, half_dim):
    frequency = 10000.0 ** (-jnp.arange(half_dim, dtype=jnp.float32) / half_dim)
    angles = pos.astype(jnp.float32)[:, None] * frequency[None, :]
    cosine = jnp.cos(angles)[:, None, :]
    sine_part = jnp.sin(angles)[:, None, :]
    front_part = x[..., :half_dim]
    back_part = x[..., half_dim:]
    return jnp.concatenate(
        [front_part * cosine - back_part * sine_part, back_part * cosine + front_part * sine_part],
        axis=-1,
    )


def make_attend(query_rot, tquery_rot, query_ids, scale):

    def attend(carry, block):
        best, total, weighted, primal_acc, slope_acc, spread_acc = carry
        key_blk, value_blk, tkey_blk, tvalue_blk, key_ids = block
        scores = (
            jnp.einsum("hqd,hkd->hqk", query_rot, key_blk, preferred_element_type=jnp.float32)
            * scale
        )
        same_clip = query_ids[:, None] == key_ids[None, :]
        scores = jnp.where(same_clip[None], scores, -jnp.inf)
        slopes = (
            jnp.einsum("hqd,hkd->hqk", tquery_rot, key_blk, preferred_element_type=jnp.float32)
            + jnp.einsum("hqd,hkd->hqk", query_rot, tkey_blk, preferred_element_type=jnp.float32)
        ) * scale
        new_best = jnp.maximum(best, jnp.max(scores, axis=-1))
        factor = jnp.exp(best - new_best)
        weights = jnp.exp(scores - new_best[..., None])
        tilted = weights * slopes
        total = total * factor + jnp.sum(weights, axis=-1)
        weighted = weighted * factor + jnp.sum(tilted, axis=-1)
        weights_b = weights.astype(jnp.bfloat16)
        tilted_b = tilted.astype(jnp.bfloat16)
        primal_acc = primal_acc * factor[..., None] + jnp.einsum(
            "hqk,hkd->hqd", weights_b, value_blk, preferred_element_type=jnp.float32
        )
        slope_acc = slope_acc * factor[..., None] + jnp.einsum(
            "hqk,hkd->hqd", tilted_b, value_blk, preferred_element_type=jnp.float32
        )
        spread_acc = spread_acc * factor[..., None] + jnp.einsum(
            "hqk,hkd->hqd", weights_b, tvalue_blk, preferred_element_type=jnp.float32
        )
        return ((new_best, total, weighted, primal_acc, slope_acc, spread_acc), None)

    return attend


def start_states(heads, rows, head_dim):
    zeros_rows = jnp.zeros((heads, rows), jnp.float32)
    zeros_heads = jnp.zeros((heads, rows, head_dim), jnp.float32)
    return (
        jnp.full((heads, rows), -1e30, jnp.float32),
        zeros_rows,
        zeros_rows,
        zeros_heads,
        zeros_heads,
        zeros_heads,
    )


def local(
    queries,
    keys,
    values,
    tangent_queries,
    tangent_keys,
    tangent_values,
    clip_ids,
    block_order,
    out_weight,
    layer_scale,
    cotangent,
):
    tok_rows = queries.shape[1]
    heads = HEADS
    head_dim = queries.shape[2] // heads
    scale = head_dim ** (-0.5)
    cycle_index = lax.axis_index("ctx")
    positions = block_order[cycle_index] * tok_rows + jnp.arange(tok_rows, dtype=jnp.int32)

    def heads_first(x, turned):
        y = x[0].reshape(tok_rows, heads, head_dim)
        if turned:
            y = rotate(y.astype(jnp.float32), positions, head_dim // 2).astype(jnp.bfloat16)
        return jnp.transpose(y, (1, 0, 2))

    query_rot = heads_first(queries, True)
    key_rot = heads_first(keys, True)
    value_heads = heads_first(values, False)
    tquery_rot = heads_first(tangent_queries, True)
    tkey_rot = heads_first(tangent_keys, True)
    tvalue_heads = heads_first(tangent_values, False)
    all_ids = lax.all_gather(clip_ids, "ctx", axis=1, tiled=True)[0]
    own_ids = clip_ids[0]
    attend = make_attend(query_rot, tquery_rot, own_ids, scale)
    carry = start_states(heads, tok_rows, head_dim)
    key_part = lax.all_gather(key_rot, "ctx", axis=1, tiled=True)
    value_part = lax.all_gather(value_heads, "ctx", axis=1, tiled=True)
    tkey_part = lax.all_gather(tkey_rot, "ctx", axis=1, tiled=True)
    tvalue_part = lax.all_gather(tvalue_heads, "ctx", axis=1, tiled=True)
    count = key_part.shape[1]
    block_rows = math.gcd(count, tok_rows)
    blocks = count // block_rows

    def split_blocks(x):
        return jnp.transpose(x.reshape(heads, blocks, block_rows, head_dim), (1, 0, 2, 3))

    stacked = (
        split_blocks(key_part),
        split_blocks(value_part),
        split_blocks(tkey_part),
        split_blocks(tvalue_part),
        all_ids.reshape(blocks, block_rows),
    )
    carry, unused = lax.scan(attend, carry, stacked)
    best, total, weighted, primal_acc, slope_acc, spread_acc = carry
    mean_out = primal_acc / total[..., None]
    tangent_heads = (
        (slope_acc + spread_acc) / total[..., None] - (weighted / total)[..., None] * mean_out
    ).astype(jnp.bfloat16)
    tangent_rows = jnp.transpose(tangent_heads, (1, 0, 2)).reshape(tok_rows, heads * head_dim)
    projected = jnp.dot(tangent_rows, out_weight, preferred_element_type=jnp.float32)
    branch = (layer_scale * projected).astype(jnp.bfloat16)[None]
    partial_grad = jnp.sum(cotangent[0].astype(jnp.float32) * projected, axis=0)
    summed = lax.psum(partial_grad, ("ctx", "dp"))
    count_all = lax.axis_size("ctx") * lax.axis_size("dp") * tok_rows
    return (branch, summed / math.sqrt(count_all))


def solution(mesh):
    in_specs = (
        P("dp", "ctx", None),
        P("dp", "ctx", None),
        P("dp", "ctx", None),
        P("dp", "ctx", None),
        P("dp", "ctx", None),
        P("dp", "ctx", None),
        P("dp", "ctx"),
        P(),
        P(),
        P(),
        P("dp", "ctx", None),
    )
    out_specs = (P("dp", "ctx", None), P())
    return jax.shard_map(local, mesh=mesh, in_specs=in_specs, out_specs=out_specs, check_vma=False)
```

profile of v0, /device:TPU:1, one launch (start us, length us, event | category | flops | bytes accessed | tf_op | source)
XLA Modules:
  0.0 623.5 jit_solution(16415383374081786712)
XLA Ops:
  18.6 1.9 copy.28
  22.8 25.8 %all_gather.15 = s32[1,2048]{1,0:T(1,128)} all-gather(s32[1,128]{1,0:T(1,128)} %param.19), channel_id=1, replica_groups=mesh['ctx'=16,'dp'=16] {'ctx'}, dimensions={1}, use_global_device_ids=true | all-gather | bytes 8704 | tf_op jit(solution)/shard_map/all_gather | solution.py:105
  48.7 46.9 %all-gather.5.cloned.1.call-done = bf16[12,2048,128]{1,2,0:T(8,128)(2,1)} async-done(((bf16[12,128,128]{1,2,0:T(8,128)(2,1)}), bf16[12,2048,128]{1,2,0:T(8,128)(2,1)}) %all-gather.5.cloned.1.call-update) | async-done | bytes 6291472 | tf_op jit(solution)/shard_map/all_gather | solution.py:109
  95.6 7.8 %copy.44 = bf16[192,8,16,128]{3,2,1,0:T(8,128)(2,1)} copy(bf16[192,8,16,128]{3,1,2,0:T(8,128)(2,1)} %bitcast.120) | data formatting | bytes 12582912
  103.3 9.0 %copy.21 = bf16[12,16,128,128]{3,2,0,1:T(8,128)(2,1)} copy(bf16[12,16,128,128]{2,1,3,0:T(8,128)(2,1)} %bitcast.115) | data formatting | bytes 12582912 | tf_op jit(solution)/shard_map/reshape | solution.py:118
  112.4 58.9 %all-gather.7.cloned.1.call-done = bf16[12,2048,128]{1,2,0:T(8,128)(2,1)} async-done(((bf16[12,128,128]{1,2,0:T(8,128)(2,1)}), bf16[12,2048,128]{1,2,0:T(8,128)(2,1)}) %all-gather.7.cloned.1.call-update) | async-done | bytes 6291472 | tf_op jit(solution)/shard_map/all_gather | solution.py:111
  171.3 8.7 %copy.25 = bf16[12,2048,128]{2,1,0:T(8,128)(2,1)} copy(bf16[12,2048,128]{1,2,0:T(8,128)(2,1)} %all-gather.7.cloned.1.call-done) | data formatting | bytes 12582912 | tf_op jit(solution)/shard_map/all_gather | solution.py:111
  180.0 67.1 %all-gather.9.cloned.1.call-done = bf16[12,2048,128]{1,2,0:T(8,128)(2,1)} async-done(((bf16[12,128,128]{1,2,0:T(8,128)(2,1)}), bf16[12,2048,128]{1,2,0:T(8,128)(2,1)}) %all-gather.9.cloned.1.call-update) | async-done | bytes 6291472 | tf_op jit(solution)/shard_map/all_gather | solution.py:110
  247.1 8.6 %copy.27 = bf16[12,2048,128]{2,1,0:T(8,128)(2,1)} copy(bf16[12,2048,128]{1,2,0:T(8,128)(2,1)} %all-gather.9.cloned.1.call-done) | data formatting | bytes 12582912 | tf_op jit(solution)/shard_map/all_gather | solution.py:110
  255.7 67.0 %all-gather.11.cloned.1.call-done = bf16[12,2048,128]{1,2,0:T(8,128)(2,1)} async-done(((bf16[12,128,128]{1,2,0:T(8,128)(2,1)}), bf16[12,2048,128]{1,2,0:T(8,128)(2,1)}) %all-gather.11.cloned.1.call-update) | async-done | bytes 6291472 | tf_op jit(solution)/shard_map/all_gather | solution.py:112
  322.7 8.7 %copy.29 = bf16[12,2048,128]{2,1,0:T(8,128)(2,1)} copy(bf16[12,2048,128]{1,2,0:T(8,128)(2,1)} %all-gather.11.cloned.1.call-done) | data formatting | bytes 12582912 | tf_op jit(solution)/shard_map/all_gather | solution.py:112
  331.3 200.5 %while.21 = (s32[]{:T(128)}, f32[12,128]{1,0:T(8,128)S(1)}, f32[12,128]{1,0:T(8,128)}, f32[12,128]{1,0:T(8,128)}, f32[12,128,128]{2,1,0:T(8,128)S(1)}, /*index=5...) while((s32[]{:T(128)}, f32[12,128]{1,0:T(8,128)S(1)}, ...), condition=%wide.region_4.5_spmd.clone, body=%wide.region_0.4_spmd.clone.sunk | while | flops 306735616 | bytes 14789864 | solution.py:127
  353.5 1.6 convolution_add_fusion.7
  378.6 1.6 convolution_add_fusion.7
  403.8 1.6 convolution_add_fusion.7
  441.5 1.6 convolution_add_fusion.7
  454.1 1.6 convolution_add_fusion.7
  466.6 1.6 convolution_add_fusion.7
  491.8 1.6 convolution_add_fusion.7
  504.3 1.6 convolution_add_fusion.7
  516.9 1.6 convolution_add_fusion.7
  529.5 1.6 convolution_add_fusion.7
  534.3 6.4 %fusion.32 = (f32[3072]{0:T(1024)S(1)}, bf16[1,128,3072]{2,1,0:T(8,128)(2,1)}) fusion(bf16[1,128,3072]{2,1,0:T(8,128)(2,1)} %param.23, f32[3072]{0:T(1024)S(1)} %copy-done.3, bf16[128,1536]{0,1:T(8,128)(2,1)S(1)} %bitcast.121, bf16[1536,3072]{1,0:T(8,128)(2,1)} %param.21), kind=kOutput, calls=%fused_computation.46 | convolution fusion | flops 1209922560 | bytes 11427840 | tf_op jit(solution)/shard_map/dot_general | solution.py:134
  540.7 75.7 %psum.7 = f32[3072]{0:T(1024)S(1)} all-reduce(f32[3072]{0:T(1024)S(1)} %get-tuple-element.187), channel_id=1, replica_groups=mesh['ctx'=16,'dp'=16] {'ctx','dp'}, use_global_device_ids=true, to_apply=%region_6.7 | all-reduce | flops 3072 | bytes 24576 | tf_op jit(solution)/shard_map/psum | solution.py:137
  (305 shorter events, 198.9 us)
Async XLA Ops:
  7.2 88.4 %all-gather.5.cloned.1.call-start = ((), (), s32[]{:S(2)}) async-start(), calls=%async_computation | async-start | bytes 6684672 | tf_op jit(solution)/shard_map/all_gather | solution.py:109
  11.7 5.9 copy-start.2
  16.6 154.7 %all-gather.7.cloned.1.call-start = ((), (), s32[]{:S(2)}) async-start(), calls=%async_computation.1 | async-start | bytes 6684672 | tf_op jit(solution)/shard_map/all_gather | solution.py:111
  17.5 229.6 %all-gather.9.cloned.1.call-start = ((), (), s32[]{:S(2)}) async-start(), calls=%async_computation.2 | async-start | bytes 6684672 | tf_op jit(solution)/shard_map/all_gather | solution.py:110
  18.5 304.1 %all-gather.11.cloned.1.call-start = ((), (), s32[]{:S(2)}) async-start(), calls=%async_computation.3 | async-start | bytes 6684672 | tf_op jit(solution)/shard_map/all_gather | solution.py:112
  334.2 8.4 %copy-start = (f32[12,128]{1,0:T(8,128)S(1)}, f32[12,128]{1,0:T(8,128)}, u32[]{:S(2)}) copy-start(f32[12,128]{1,0:T(8,128)} %get-tuple-element.331) | copy-start | bytes 18436 | tf_op jit(solution)/shard_map/while
  346.1 9.1 %copy-start = (f32[12,128]{1,0:T(8,128)S(1)}, f32[12,128]{1,0:T(8,128)}, u32[]{:S(2)}) copy-start(f32[12,128]{1,0:T(8,128)} %get-tuple-element.331) | copy-start | bytes 18436 | tf_op jit(solution)/shard_map/while
  355.2 0.6 copy-start.1
  358.6 9.1 %copy-start = (f32[12,128]{1,0:T(8,128)S(1)}, f32[12,128]{1,0:T(8,128)}, u32[]{:S(2)}) copy-start(f32[12,128]{1,0:T(8,128)} %get-tuple-element.331) | copy-start | bytes 18436 | tf_op jit(solution)/shard_map/while
  367.8 0.6 copy-start.1
  371.2 9.1 %copy-start = (f32[12,128]{1,0:T(8,128)S(1)}, f32[12,128]{1,0:T(8,128)}, u32[]{:S(2)}) copy-start(f32[12,128]{1,0:T(8,128)} %get-tuple-element.331) | copy-start | bytes 18436 | tf_op jit(solution)/shard_map/while
  383.8 9.1 %copy-start = (f32[12,128]{1,0:T(8,128)S(1)}, f32[12,128]{1,0:T(8,128)}, u32[]{:S(2)}) copy-start(f32[12,128]{1,0:T(8,128)} %get-tuple-element.331) | copy-start | bytes 18436 | tf_op jit(solution)/shard_map/while
  396.4 9.1 %copy-start = (f32[12,128]{1,0:T(8,128)S(1)}, f32[12,128]{1,0:T(8,128)}, u32[]{:S(2)}) copy-start(f32[12,128]{1,0:T(8,128)} %get-tuple-element.331) | copy-start | bytes 18436 | tf_op jit(solution)/shard_map/while
  408.9 9.1 %copy-start = (f32[12,128]{1,0:T(8,128)S(1)}, f32[12,128]{1,0:T(8,128)}, u32[]{:S(2)}) copy-start(f32[12,128]{1,0:T(8,128)} %get-tuple-element.331) | copy-start | bytes 18436 | tf_op jit(solution)/shard_map/while
  421.5 9.1 %copy-start = (f32[12,128]{1,0:T(8,128)S(1)}, f32[12,128]{1,0:T(8,128)}, u32[]{:S(2)}) copy-start(f32[12,128]{1,0:T(8,128)} %get-tuple-element.331) | copy-start | bytes 18436 | tf_op jit(solution)/shard_map/while
  434.1 9.1 %copy-start = (f32[12,128]{1,0:T(8,128)S(1)}, f32[12,128]{1,0:T(8,128)}, u32[]{:S(2)}) copy-start(f32[12,128]{1,0:T(8,128)} %get-tuple-element.331) | copy-start | bytes 18436 | tf_op jit(solution)/shard_map/while
  446.7 9.1 %copy-start = (f32[12,128]{1,0:T(8,128)S(1)}, f32[12,128]{1,0:T(8,128)}, u32[]{:S(2)}) copy-start(f32[12,128]{1,0:T(8,128)} %get-tuple-element.331) | copy-start | bytes 18436 | tf_op jit(solution)/shard_map/while
  459.2 9.1 %copy-start = (f32[12,128]{1,0:T(8,128)S(1)}, f32[12,128]{1,0:T(8,128)}, u32[]{:S(2)}) copy-start(f32[12,128]{1,0:T(8,128)} %get-tuple-element.331) | copy-start | bytes 18436 | tf_op jit(solution)/shard_map/while
  471.8 9.1 %copy-start = (f32[12,128]{1,0:T(8,128)S(1)}, f32[12,128]{1,0:T(8,128)}, u32[]{:S(2)}) copy-start(f32[12,128]{1,0:T(8,128)} %get-tuple-element.331) | copy-start | bytes 18436 | tf_op jit(solution)/shard_map/while
  484.4 9.1 %copy-start = (f32[12,128]{1,0:T(8,128)S(1)}, f32[12,128]{1,0:T(8,128)}, u32[]{:S(2)}) copy-start(f32[12,128]{1,0:T(8,128)} %get-tuple-element.331) | copy-start | bytes 18436 | tf_op jit(solution)/shard_map/while
  496.9 9.1 %copy-start = (f32[12,128]{1,0:T(8,128)S(1)}, f32[12,128]{1,0:T(8,128)}, u32[]{:S(2)}) copy-start(f32[12,128]{1,0:T(8,128)} %get-tuple-element.331) | copy-start | bytes 18436 | tf_op jit(solution)/shard_map/while
  509.5 9.1 %copy-start = (f32[12,128]{1,0:T(8,128)S(1)}, f32[12,128]{1,0:T(8,128)}, u32[]{:S(2)}) copy-start(f32[12,128]{1,0:T(8,128)} %get-tuple-element.331) | copy-start | bytes 18436 | tf_op jit(solution)/shard_map/while
  522.1 9.1 %copy-start = (f32[12,128]{1,0:T(8,128)S(1)}, f32[12,128]{1,0:T(8,128)}, u32[]{:S(2)}) copy-start(f32[12,128]{1,0:T(8,128)} %get-tuple-element.331) | copy-start | bytes 18436 | tf_op jit(solution)/shard_map/while
  531.8 2.5 copy-start.3
  (14 other events, 8.4 us)
Sparse Core Ops, SparseCore 0:
  16.7 78.7 all-gather.4
  98.1 73.1 all-gather.6
  173.9 73.1 all-gather.8
  249.5 73.1 all-gather.10
where the time goes:
time: 630 us; the launch traced here: 623 us
  waiting for transfers between devices  240 us (38%)
  matrix products  150 us (24%)
  blocking collectives  102 us (16%)
  local copies, waits for them, and re-layouts  74 us (12%)
  other arithmetic  41 us (7%)
  between operations  14.6 us (2%)
    psum x1, blocking collectives, local(): summed = lax.psum(partial_grad, ('ctx', 'dp'))  75.7 us
    all_gather x1, waiting for transfers between devices, local(): value_part = lax.all_gather(value_heads, 'ctx', axis=1, tiled=True)  67.1 us
    all_gather x1, waiting for transfers between devices, local(): tvalue_part = lax.all_gather(tvalue_heads, 'ctx', axis=1, tiled=True)  67 us
    all_gather x1, waiting for transfers between devices, local(): tkey_part = lax.all_gather(tkey_rot, 'ctx', axis=1, tiled=True)  58.9 us
    all_gather x1, waiting for transfers between devices, local(): key_part = lax.all_gather(key_rot, 'ctx', axis=1, tiled=True)  46.9 us
    all_gather x1, blocking collectives, local(): all_ids = lax.all_gather(clip_ids, 'ctx', axis=1, tiled=True)[0]  25.8 us
    dot_general x16, matrix products, attend(): jnp.einsum('hqk,hkd->hqd', weights_b, value_blk, preferred_element_type=j...  25.1 us
    dot_general x16, matrix products, attend(): jnp.einsum('hqk,hkd->hqd', tilted_b, value_blk, preferred_element_type=jn...  24.9 us
  transfers between devices with their start and end apart: 4, of which 4 were waited for; matrix products, arithmetic and copies ran while one was open for 6% of the time, Pallas kernels for 0%

commit v1 on v0

--- a/solution.py
+++ b/solution.py
@@ -109,7 +109,9 @@
     key_part = lax.all_gather(key_rot, "ctx", axis=1, tiled=True)
     value_part = lax.all_gather(value_heads, "ctx", axis=1, tiled=True)
     tkey_part = lax.all_gather(tkey_rot, "ctx", axis=1, tiled=True)
-    tvalue_part = lax.all_gather(tvalue_heads, "ctx", axis=1, tiled=True)
+    tvalue_part = jnp.concatenate(
+        lax.all_to_all(jnp.stack([tvalue_heads] * lax.axis_size("ctx")), "ctx", 0, 0), axis=1
+    )
     count = key_part.shape[1]
     block_rows = math.gcd(count, tok_rows)
     blocks = count // block_rows

time: 630 us -> 604 us (0.959)
  waiting for transfers between devices: 240 us -> 138 us
  blocking collectives: 102 us -> 174 us
  starting transfers between devices: 0.16 us -> 8.57 us
    all_gather x1, blocking collectives: 25.8 us -> 98.7 us  [local(): all_ids = lax.all_gather(clip_ids, 'ctx', axis=1, tiled=True)[0]]
    all_gather x1 -> x0, waiting for transfers between devices: 67 us -> none  [local(): tvalue_part = lax.all_gather(tvalue_heads, 'ctx', axis=1, tiled=True)]
    all_gather x1, waiting for transfers between devices: 46.9 us -> 13 us  [local(): key_part = lax.all_gather(key_rot, 'ctx', axis=1, tiled=True)]
    all_gather x1 -> x0, local copies, waits for them, and re-layouts: 8.67 us -> none  [local(): tvalue_part = lax.all_gather(tvalue_heads, 'ctx', axis=1, tiled=True)]
    all_to_all x0 -> x1, starting transfers between devices: none -> 8.45 us  [local(): lax.all_to_all(jnp.stack([tvalue_heads] * lax.axis_size('ctx')), 'ctx', 0...]
  transfers between devices with their start and end apart: 4 -> 4, of which waited for: 4 -> 3; matrix products, arithmetic and copies ran while one was open for 6% -> 7% of each run, Pallas kernels for 0% -> 0%
where the time goes in v1:
time: 604 us; the launch traced here: 598 us
  blocking collectives  174 us (29%)
  matrix products  150 us (25%)
  waiting for transfers between devices  138 us (23%)
  local copies, waits for them, and re-layouts  69.3 us (11%)
  other arithmetic  41 us (7%)
  between operations  14.6 us (2%)
  starting transfers between devices  8.57 us (1%)
    all_gather x1, blocking collectives, local(): all_ids = lax.all_gather(clip_ids, 'ctx', axis=1, tiled=True)[0]  98.7 us
    psum x1, blocking collectives, local(): summed = lax.psum(partial_grad, ('ctx', 'dp'))  75.7 us
    all_gather x1, waiting for transfers between devices, local(): value_part = lax.all_gather(value_heads, 'ctx', axis=1, tiled=True)  67.2 us
    all_gather x1, waiting for transfers between devices, local(): tkey_part = lax.all_gather(tkey_rot, 'ctx', axis=1, tiled=True)  58.2 us
    dot_general x16, matrix products, attend(): jnp.einsum('hqk,hkd->hqd', weights_b, value_blk, preferred_element_type=j...  25.1 us
    dot_general x16, matrix products, attend(): jnp.einsum('hqk,hkd->hqd', tilted_b, value_blk, preferred_element_type=jn...  24.9 us
    dot_general x16, matrix products, attend(): jnp.einsum('hqk,hkd->hqd', weights_b, tvalue_blk, preferred_element_type=...  24.8 us
    dot_general x16, matrix products, attend(): jnp.einsum('hqd,hkd->hqk', tquery_rot, key_blk, preferred_element_type=jn...  24.1 us
  transfers between devices with their start and end apart: 4, of which 3 were waited for; matrix products, arithmetic and copies ran while one was open for 7% of the time, Pallas kernels for 0%

profile of v1, /device:TPU:1, one launch (start us, length us, event | category | flops | bytes accessed | tf_op | source)
XLA Modules:
  0.0 598.3 jit_solution(16564892859626204754)
XLA Ops:
  20.0 4.3 stack.2
  24.3 8.4 %all-to-all-start = ((bf16[16,12,128,128]{3,2,1,0:T(8,128)(2,1)}), bf16[16,12,128,128]{3,2,1,0:T(8,128)(2,1)}, u32[]{:S(2)}, u32[]{:S(2)}) async-start(bf16[16,12,128,128]{3,2,1,0:T(8,128)(2,1)} %stack.2), calls=%async_computation | async-start | bytes 12582912 | tf_op jit(solution)/shard_map/all_to_all | solution.py:113
  35.1 98.7 %all_gather.12 = s32[1,2048]{1,0:T(1,128)} all-gather(s32[1,128]{1,0:T(1,128)} %param.19), channel_id=1, replica_groups=mesh['ctx'=16,'dp'=16] {'ctx'}, dimensions={1}, use_global_device_ids=true | all-gather | bytes 8704 | tf_op jit(solution)/shard_map/all_gather | solution.py:105
  133.8 13.0 %all-gather.4.cloned.1.call-done = bf16[12,2048,128]{1,2,0:T(8,128)(2,1)} async-done(((bf16[12,128,128]{1,2,0:T(8,128)(2,1)}), bf16[12,2048,128]{1,2,0:T(8,128)(2,1)}) %all-gather.4.cloned.1.call-update) | async-done | bytes 6291472 | tf_op jit(solution)/shard_map/all_gather | solution.py:109
  146.8 7.7 %copy.43 = bf16[192,8,16,128]{3,2,1,0:T(8,128)(2,1)} copy(bf16[192,8,16,128]{3,1,2,0:T(8,128)(2,1)} %bitcast.114) | data formatting | bytes 12582912
  154.5 9.0 %copy.22 = bf16[12,16,128,128]{3,2,0,1:T(8,128)(2,1)} copy(bf16[12,16,128,128]{2,1,3,0:T(8,128)(2,1)} %bitcast.110) | data formatting | bytes 12582912 | tf_op jit(solution)/shard_map/reshape | solution.py:120
  163.5 58.2 %all-gather.6.cloned.1.call-done = bf16[12,2048,128]{1,2,0:T(8,128)(2,1)} async-done(((bf16[12,128,128]{1,2,0:T(8,128)(2,1)}), bf16[12,2048,128]{1,2,0:T(8,128)(2,1)}) %all-gather.6.cloned.1.call-update) | async-done | bytes 6291472 | tf_op jit(solution)/shard_map/all_gather | solution.py:111
  221.7 8.6 %copy.26 = bf16[12,2048,128]{2,1,0:T(8,128)(2,1)} copy(bf16[12,2048,128]{1,2,0:T(8,128)(2,1)} %all-gather.6.cloned.1.call-done) | data formatting | bytes 12582912 | tf_op jit(solution)/shard_map/all_gather | solution.py:111
  230.3 67.2 %all-gather.8.cloned.1.call-done = bf16[12,2048,128]{1,2,0:T(8,128)(2,1)} async-done(((bf16[12,128,128]{1,2,0:T(8,128)(2,1)}), bf16[12,2048,128]{1,2,0:T(8,128)(2,1)}) %all-gather.8.cloned.1.call-update) | async-done | bytes 6291472 | tf_op jit(solution)/shard_map/all_gather | solution.py:110
  297.5 8.7 %copy.28 = bf16[12,2048,128]{2,1,0:T(8,128)(2,1)} copy(bf16[12,2048,128]{1,2,0:T(8,128)(2,1)} %all-gather.8.cloned.1.call-done) | data formatting | bytes 12582912 | tf_op jit(solution)/shard_map/all_gather | solution.py:110
  306.2 200.5 %while.21 = (s32[]{:T(128)}, f32[12,128]{1,0:T(8,128)S(1)}, f32[12,128]{1,0:T(8,128)}, f32[12,128]{1,0:T(8,128)}, f32[12,128,128]{2,1,0:T(8,128)S(1)}, /*index=5...) while((s32[]{:T(128)}, f32[12,128]{1,0:T(8,128)S(1)}, ...), condition=%wide.region_4.5_spmd.clone, body=%wide.region_0.4_spmd.clone.sunk | while | flops 306735616 | bytes 14789864 | solution.py:129
  315.8 1.6 convolution_add_fusion.7
  328.3 1.6 convolution_add_fusion.7
  340.9 1.6 convolution_add_fusion.7
  353.5 1.6 convolution_add_fusion.7
  366.1 1.6 convolution_add_fusion.7
  378.6 1.6 convolution_add_fusion.7
  391.2 1.6 convolution_add_fusion.7
  403.8 1.6 convolution_add_fusion.7
  416.3 1.6 convolution_add_fusion.7
  441.5 1.6 convolution_add_fusion.7
  479.2 1.6 convolution_add_fusion.7
  509.2 6.4 %fusion.32 = (f32[3072]{0:T(1024)S(1)}, bf16[1,128,3072]{2,1,0:T(8,128)(2,1)}) fusion(bf16[1,128,3072]{2,1,0:T(8,128)(2,1)} %param.23, f32[3072]{0:T(1024)S(1)} %copy-done.3, bf16[128,1536]{0,1:T(8,128)(2,1)S(1)} %bitcast.115, bf16[1536,3072]{1,0:T(8,128)(2,1)} %param.21), kind=kOutput, calls=%fused_computation.46 | convolution fusion | flops 1209922560 | bytes 11427840 | tf_op jit(solution)/shard_map/dot_general | solution.py:136
  515.5 75.7 %psum.7 = f32[3072]{0:T(1024)S(1)} all-reduce(f32[3072]{0:T(1024)S(1)} %get-tuple-element.187), channel_id=1, replica_groups=mesh['ctx'=16,'dp'=16] {'ctx','dp'}, use_global_device_ids=true, to_apply=%region_6.7 | all-reduce | flops 3072 | bytes 24576 | tf_op jit(solution)/shard_map/psum | solution.py:139
  (305 shorter events, 198.8 us)
Async XLA Ops:
  7.2 139.6 %all-gather.4.cloned.1.call-start = ((), (), s32[]{:S(2)}) async-start(), calls=%async_computation.1 | async-start | bytes 6684672 | tf_op jit(solution)/shard_map/all_gather | solution.py:109
  11.7 5.9 copy-start.2
  16.6 205.1 %all-gather.6.cloned.1.call-start = ((), (), s32[]{:S(2)}) async-start(), calls=%async_computation.2 | async-start | bytes 6684672 | tf_op jit(solution)/shard_map/all_gather | solution.py:111
  17.5 280.0 %all-gather.8.cloned.1.call-start = ((), (), s32[]{:S(2)}) async-start(), calls=%async_computation.3 | async-start | bytes 6684672 | tf_op jit(solution)/shard_map/all_gather | solution.py:110
  24.3 281.9 %all-to-all-start = ((bf16[16,12,128,128]{3,2,1,0:T(8,128)(2,1)}), bf16[16,12,128,128]{3,2,1,0:T(8,128)(2,1)}, u32[]{:S(2)}, u32[]{:S(2)}) async-start(bf16[16,12,128,128]{3,2,1,0:T(8,128)(2,1)} %stack.2), calls=%async_computation | async-start | bytes 12582912 | tf_op jit(solution)/shard_map/all_to_all | solution.py:113
  309.1 8.4 %copy-start = (f32[12,128]{1,0:T(8,128)S(1)}, f32[12,128]{1,0:T(8,128)}, u32[]{:S(2)}) copy-start(f32[12,128]{1,0:T(8,128)} %get-tuple-element.331) | copy-start | bytes 18436 | tf_op jit(solution)/shard_map/while
  320.9 9.1 %copy-start = (f32[12,128]{1,0:T(8,128)S(1)}, f32[12,128]{1,0:T(8,128)}, u32[]{:S(2)}) copy-start(f32[12,128]{1,0:T(8,128)} %get-tuple-element.331) | copy-start | bytes 18436 | tf_op jit(solution)/shard_map/while
  333.5 9.1 %copy-start = (f32[12,128]{1,0:T(8,128)S(1)}, f32[12,128]{1,0:T(8,128)}, u32[]{:S(2)}) copy-start(f32[12,128]{1,0:T(8,128)} %get-tuple-element.331) | copy-start | bytes 18436 | tf_op jit(solution)/shard_map/while
  342.6 0.6 copy-start.1
  346.1 9.1 %copy-start = (f32[12,128]{1,0:T(8,128)S(1)}, f32[12,128]{1,0:T(8,128)}, u32[]{:S(2)}) copy-start(f32[12,128]{1,0:T(8,128)} %get-tuple-element.331) | copy-start | bytes 18436 | tf_op jit(solution)/shard_map/while
  355.2 0.6 copy-start.1
  358.7 9.1 %copy-start = (f32[12,128]{1,0:T(8,128)S(1)}, f32[12,128]{1,0:T(8,128)}, u32[]{:S(2)}) copy-start(f32[12,128]{1,0:T(8,128)} %get-tuple-element.331) | copy-start | bytes 18436 | tf_op jit(solution)/shard_map/while
  371.2 9.1 %copy-start = (f32[12,128]{1,0:T(8,128)S(1)}, f32[12,128]{1,0:T(8,128)}, u32[]{:S(2)}) copy-start(f32[12,128]{1,0:T(8,128)} %get-tuple-element.331) | copy-start | bytes 18436 | tf_op jit(solution)/shard_map/while
  383.8 9.1 %copy-start = (f32[12,128]{1,0:T(8,128)S(1)}, f32[12,128]{1,0:T(8,128)}, u32[]{:S(2)}) copy-start(f32[12,128]{1,0:T(8,128)} %get-tuple-element.331) | copy-start | bytes 18436 | tf_op jit(solution)/shard_map/while
  396.4 9.1 %copy-start = (f32[12,128]{1,0:T(8,128)S(1)}, f32[12,128]{1,0:T(8,128)}, u32[]{:S(2)}) copy-start(f32[12,128]{1,0:T(8,128)} %get-tuple-element.331) | copy-start | bytes 18436 | tf_op jit(solution)/shard_map/while
  409.0 9.1 %copy-start = (f32[12,128]{1,0:T(8,128)S(1)}, f32[12,128]{1,0:T(8,128)}, u32[]{:S(2)}) copy-start(f32[12,128]{1,0:T(8,128)} %get-tuple-element.331) | copy-start | bytes 18436 | tf_op jit(solution)/shard_map/while
  421.5 9.1 %copy-start = (f32[12,128]{1,0:T(8,128)S(1)}, f32[12,128]{1,0:T(8,128)}, u32[]{:S(2)}) copy-start(f32[12,128]{1,0:T(8,128)} %get-tuple-element.331) | copy-start | bytes 18436 | tf_op jit(solution)/shard_map/while
  434.1 9.1 %copy-start = (f32[12,128]{1,0:T(8,128)S(1)}, f32[12,128]{1,0:T(8,128)}, u32[]{:S(2)}) copy-start(f32[12,128]{1,0:T(8,128)} %get-tuple-element.331) | copy-start | bytes 18436 | tf_op jit(solution)/shard_map/while
  446.7 9.1 %copy-start = (f32[12,128]{1,0:T(8,128)S(1)}, f32[12,128]{1,0:T(8,128)}, u32[]{:S(2)}) copy-start(f32[12,128]{1,0:T(8,128)} %get-tuple-element.331) | copy-start | bytes 18436 | tf_op jit(solution)/shard_map/while
  459.3 9.1 %copy-start = (f32[12,128]{1,0:T(8,128)S(1)}, f32[12,128]{1,0:T(8,128)}, u32[]{:S(2)}) copy-start(f32[12,128]{1,0:T(8,128)} %get-tuple-element.331) | copy-start | bytes 18436 | tf_op jit(solution)/shard_map/while
  471.9 9.1 %copy-start = (f32[12,128]{1,0:T(8,128)S(1)}, f32[12,128]{1,0:T(8,128)}, u32[]{:S(2)}) copy-start(f32[12,128]{1,0:T(8,128)} %get-tuple-element.331) | copy-start | bytes 18436 | tf_op jit(solution)/shard_map/while
  484.4 9.1 %copy-start = (f32[12,128]{1,0:T(8,128)S(1)}, f32[12,128]{1,0:T(8,128)}, u32[]{:S(2)}) copy-start(f32[12,128]{1,0:T(8,128)} %get-tuple-element.331) | copy-start | bytes 18436 | tf_op jit(solution)/shard_map/while
  497.0 9.1 %copy-start = (f32[12,128]{1,0:T(8,128)S(1)}, f32[12,128]{1,0:T(8,128)}, u32[]{:S(2)}) copy-start(f32[12,128]{1,0:T(8,128)} %get-tuple-element.331) | copy-start | bytes 18436 | tf_op jit(solution)/shard_map/while
  506.7 2.5 copy-start.3
  (14 other events, 8.4 us)
Sparse Core Ops, SparseCore 0:
  16.7 129.9 all-gather.3
  149.3 72.3 all-gather.5
  224.3 73.1 all-gather.7
